TPU v7x, 32 devices: a whole 2x2x4 slice. The times are simulated.
32 devices in a mesh: fsdp: 32 (over z, y, x, core).
Axes of the slice: x: 2, y: 2, z: 4, core: 2. Of those that a mesh axis runs over, the one named last changes fastest.
Arguments:
- inputs: bfloat16 [4096, 1024], P('fsdp'), may hold values from -9 to 9
- live_keys: int32 [4096], P('fsdp'), may hold values from 0 to 1, as said below
- triple_weight: bfloat16 [1024, 3072], P('fsdp'), may hold values from -1 to 1
- query_bias: bfloat16 [1024], P('fsdp'), may hold values from -3 to 3
- value_bias: bfloat16 [1024], P('fsdp'), may hold values from -3 to 3
- output_weight: bfloat16 [1024, 1024], P('fsdp'), may hold values from -1.5 to 1.5
- output_bias: bfloat16 [1024], P('fsdp'), may hold values from -3 to 3
- first_gain: bfloat16 [1024], P('fsdp'), may hold values from 0.5 to 1.5
- first_shift: bfloat16 [1024], P('fsdp'), may hold values from -3 to 3
- expand_weight: bfloat16 [1024, 4096], P('fsdp'), may hold values from -0.1875 to 0.1875
- expand_bias: bfloat16 [4096], P('fsdp'), may hold values from -3 to 3
- shrink_weight: bfloat16 [4096, 1024], P('fsdp'), may hold values from -0.09375 to 0.09375
- shrink_bias: bfloat16 [1024], P('fsdp'), may hold values from -3 to 3
- second_gain: bfloat16 [1024], P('fsdp'), may hold values from 0.5 to 1.5
- second_shift: bfloat16 [1024], P('fsdp'), may hold values from -3 to 3
- cotangent: bfloat16 [4096, 1024], P('fsdp'), may hold values from -6 to 6
Outputs:
- layer_out: bfloat16 [4096, 1024], P('fsdp')
- input_grad: bfloat16 [4096, 1024], P('fsdp')
- triple_grad: float32 [1024, 3072], P('fsdp')
- query_bias_grad: float32 [1024], P('fsdp')
- value_bias_grad: float32 [1024], P('fsdp')
- output_grad: float32 [1024, 1024], P('fsdp')
- output_bias_grad: float32 [1024], P('fsdp')
- first_gain_grad: float32 [1024], P('fsdp')
- first_shift_grad: float32 [1024], P('fsdp')
- expand_grad: float32 [1024, 4096], P('fsdp')
- expand_bias_grad: float32 [4096], P('fsdp')
- shrink_grad: float32 [4096, 1024], P('fsdp')
- shrink_bias_grad: float32 [1024], P('fsdp')
- second_gain_grad: float32 [1024], P('fsdp')
- second_shift_grad: float32 [1024], P('fsdp')
Inputs may be any that keep to these rules, and one draw needn't show every extreme that they name: `live_keys`: on each device the live rows come first: 2 to 128 of its 128 rows are live, and some device has all 128 live.
All inputs are finite; a program needn't handle non-finite values.
Results may differ from a plain program's by a relative error of at most 0.013.
The roundings to bfloat16 on the way count: a program that leaves them out, or rounds other values in their place, can miss the bound.
Values may be sent and summed in bfloat16 or wider, within the bound.
A program may use at most 256 MiB of HBM per device.

v0:
```python
import jax
import jax.numpy as jnp
from jax import lax
from jax.sharding import PartitionSpec as P

HEADS = 16


EPSILON = 1e-05
NEGATIVE = -1e30
ROOT_HALF = 0.7071067811865476
INV_ROOT_TWO_PI = 0.3989422804014327


def batched(form, left, right):
    return jnp.einsum(form, left, right, preferred_element_type=jnp.float32)


def layer_norm(hidden, gain, shift):
    center = hidden - jnp.mean(hidden, axis=-1, keepdims=True)
    inv_std = lax.rsqrt(jnp.mean(center * center, axis=-1, keepdims=True) + EPSILON)
    normed = center * inv_std
    return (normed * gain.astype(jnp.float32) + shift.astype(jnp.float32), normed, inv_std)


def layer_norm_back(upstream, normed, inv_std, gain):
    scaled = upstream * gain.astype(jnp.float32)
    inner = (
        scaled
        - jnp.mean(scaled, axis=-1, keepdims=True)
        - normed * jnp.mean(scaled * normed, axis=-1, keepdims=True)
    )
    return (inv_std * inner, jnp.sum(upstream * normed, axis=0), jnp.sum(upstream, axis=0))


def normal_cdf(values):
    return 0.5 * (1.0 + lax.erf(values * ROOT_HALF))


def masked_scores(query, keys, live):
    scores = batched("qhd,khd->hqk", query, keys)
    allowed = live == 1
    return jnp.where(allowed[None, None, :], scores, NEGATIVE)


def forward(params, tokens, live):
    (
        triple_weight,
        query_bias,
        value_bias,
        output_weight,
        output_bias,
        first_gain,
        first_shift,
        expand_weight,
        expand_bias,
        shrink_weight,
        shrink_bias,
        second_gain,
        second_shift,
    ) = params
    row_count = tokens.shape[0]
    width_all = tokens.shape[1]
    head_size = width_all // HEADS
    factor = head_size ** (-0.5)
    projected = jnp.dot(tokens, triple_weight, preferred_element_type=jnp.float32)
    query = ((projected[:, :width_all] + query_bias.astype(jnp.float32)) * factor).astype(
        jnp.bfloat16
    )
    keys = projected[:, width_all : 2 * width_all].astype(jnp.bfloat16)
    values = (projected[:, 2 * width_all :] + value_bias.astype(jnp.float32)).astype(jnp.bfloat16)
    query = query.reshape(row_count, HEADS, head_size)
    keys = keys.reshape(row_count, HEADS, head_size)
    values = values.reshape(row_count, HEADS, head_size)
    scores = masked_scores(query, keys, live)
    top = jnp.max(scores, axis=-1, keepdims=True)
    expo = jnp.exp(scores - top)
    total = jnp.sum(expo, axis=-1, keepdims=True)
    log_total = top + jnp.log(total)
    probs = (expo / total).astype(jnp.bfloat16)
    context = (
        batched("hqk,khd->qhd", probs, values).astype(jnp.bfloat16).reshape(row_count, width_all)
    )
    first_in = (
        tokens.astype(jnp.float32)
        + jnp.dot(context, output_weight, preferred_element_type=jnp.float32)
        + output_bias.astype(jnp.float32)
    )
    middle, first_norm, first_rate = layer_norm(first_in, first_gain, first_shift)
    mid_low = middle.astype(jnp.bfloat16)
    pre_act = jnp.dot(
        mid_low, expand_weight, preferred_element_type=jnp.float32
    ) + expand_bias.astype(jnp.float32)
    act_low = (pre_act * normal_cdf(pre_act)).astype(jnp.bfloat16)
    second_in = (
        middle
        + jnp.dot(act_low, shrink_weight, preferred_element_type=jnp.float32)
        + shrink_bias.astype(jnp.float32)
    )
    result, second_norm, second_rate = layer_norm(second_in, second_gain, second_shift)
    saved = (
        tokens,
        live,
        query,
        keys,
        values,
        log_total,
        context,
        first_norm,
        first_rate,
        mid_low,
        pre_act,
        act_low,
        second_norm,
        second_rate,
    )
    return (result.astype(jnp.bfloat16), saved)


def back_upper(params, saved, upstream):
    (
        triple_weight,
        query_bias,
        value_bias,
        output_weight,
        output_bias,
        first_gain,
        first_shift,
        expand_weight,
        expand_bias,
        shrink_weight,
        shrink_bias,
        second_gain,
        second_shift,
    ) = params
    (
        tokens,
        live,
        query,
        keys,
        values,
        log_total,
        context,
        first_norm,
        first_rate,
        mid_low,
        pre_act,
        act_low,
        second_norm,
        second_rate,
    ) = saved
    d_second, second_gain_grad, second_shift_grad = layer_norm_back(
        upstream.astype(jnp.float32), second_norm, second_rate, second_gain
    )
    d_second_low = d_second.astype(jnp.bfloat16)
    shrink_bias_grad = jnp.sum(d_second, axis=0)
    d_act = jnp.dot(d_second_low, shrink_weight.T, preferred_element_type=jnp.float32)
    slope = normal_cdf(pre_act) + pre_act * jnp.exp(-0.5 * pre_act * pre_act) * INV_ROOT_TWO_PI
    d_pre = d_act * slope
    expand_bias_grad = jnp.sum(d_pre, axis=0)
    d_pre_low = d_pre.astype(jnp.bfloat16)
    d_mid = d_second + jnp.dot(d_pre_low, expand_weight.T, preferred_element_type=jnp.float32)
    d_first, first_gain_grad, first_shift_grad = layer_norm_back(
        d_mid, first_norm, first_rate, first_gain
    )
    small = (
        first_gain_grad,
        first_shift_grad,
        expand_bias_grad,
        shrink_bias_grad,
        second_gain_grad,
        second_shift_grad,
    )
    pairs = ((mid_low, d_pre_low), (act_low, d_second_low))
    return (small, pairs, d_first)


def back_lower(params, saved, d_first):
    (
        triple_weight,
        query_bias,
        value_bias,
        output_weight,
        output_bias,
        first_gain,
        first_shift,
        expand_weight,
        expand_bias,
        shrink_weight,
        shrink_bias,
        second_gain,
        second_shift,
    ) = params
    (
        tokens,
        live,
        query,
        keys,
        values,
        log_total,
        context,
        first_norm,
        first_rate,
        mid_low,
        pre_act,
        act_low,
        second_norm,
        second_rate,
    ) = saved
    row_count = tokens.shape[0]
    width_all = tokens.shape[1]
    head_size = width_all // HEADS
    factor = head_size ** (-0.5)
    d_first_low = d_first.astype(jnp.bfloat16)
    output_bias_grad = jnp.sum(d_first, axis=0)
    d_context = jnp.dot(d_first_low, output_weight.T, preferred_element_type=jnp.float32).astype(
        jnp.bfloat16
    )
    d_context = d_context.reshape(row_count, HEADS, head_size)
    scores = masked_scores(query, keys, live)
    probs = jnp.exp(scores - log_total)
    probs_low = probs.astype(jnp.bfloat16)
    d_values = batched("hqk,qhd->khd", probs_low, d_context)
    d_probs = batched("qhd,khd->hqk", d_context, values)
    inner = jnp.sum(probs * d_probs, axis=-1, keepdims=True)
    d_scores = (probs * (d_probs - inner)).astype(jnp.bfloat16)
    d_query = factor * batched("hqk,khd->qhd", d_scores, keys)
    d_keys = batched("hqk,qhd->khd", d_scores, query)
    d_query = d_query.reshape(row_count, width_all)
    d_keys = d_keys.reshape(row_count, width_all)
    d_values = d_values.reshape(row_count, width_all)
    d_proj = jnp.concatenate([d_query, d_keys, d_values], axis=1).astype(jnp.bfloat16)
    query_bias_grad = jnp.sum(d_query, axis=0)
    value_bias_grad = jnp.sum(d_values, axis=0)
    input_grad = (
        d_first + jnp.dot(d_proj, triple_weight.T, preferred_element_type=jnp.float32)
    ).astype(jnp.bfloat16)
    small = (query_bias_grad, value_bias_grad, output_bias_grad)
    pairs = ((tokens, d_proj), (context, d_first_low))
    return (small, pairs, input_grad)


def owner_rows(pairs, group_size, width):
    return sum((left.shape[1] // group_size * right.shape[1] // width for left, right in pairs))


def owner_terms(pairs, group_size, width, count):
    per_owner = owner_rows(pairs, group_size, width)
    owners = count // per_owner
    pieces = []
    for left, right in pairs:
        share = left.shape[1] // group_size
        term = jnp.einsum("tk,tw->kw", left, right, preferred_element_type=jnp.float32)
        pieces.append(term.reshape(owners, share * right.shape[1] // width, width))
    return jnp.concatenate(pieces, axis=1).reshape(owners * per_owner, width)


def unpack_rows(pairs, summed, group_size, width):
    results = []
    offset = 0
    for left, right in pairs:
        share = left.shape[1] // group_size
        extent = share * right.shape[1] // width
        results.append(summed[offset : offset + extent].reshape(share, right.shape[1]))
        offset = offset + extent
    return tuple(results)


def body(
    inputs,
    live_keys,
    triple_weight,
    query_bias,
    value_bias,
    output_weight,
    output_bias,
    first_gain,
    first_shift,
    expand_weight,
    expand_bias,
    shrink_weight,
    shrink_bias,
    second_gain,
    second_shift,
    cotangent,
):
    group_size = lax.axis_size("fsdp")
    width = inputs.shape[1]
    gathered = (
        lax.all_gather(triple_weight, "fsdp", axis=0, tiled=True),
        lax.all_gather(query_bias, "fsdp", axis=0, tiled=True),
        lax.all_gather(value_bias, "fsdp", axis=0, tiled=True),
        lax.all_gather(output_weight, "fsdp", axis=0, tiled=True),
        lax.all_gather(output_bias, "fsdp", axis=0, tiled=True),
        lax.all_gather(first_gain, "fsdp", axis=0, tiled=True),
        lax.all_gather(first_shift, "fsdp", axis=0, tiled=True),
        lax.all_gather(expand_weight, "fsdp", axis=0, tiled=True),
        lax.all_gather(expand_bias, "fsdp", axis=0, tiled=True),
        lax.all_gather(shrink_weight, "fsdp", axis=0, tiled=True),
        lax.all_gather(shrink_bias, "fsdp", axis=0, tiled=True),
        lax.all_gather(second_gain, "fsdp", axis=0, tiled=True),
        lax.all_gather(second_shift, "fsdp", axis=0, tiled=True),
    )
    layer_out, saved = forward(gathered, inputs, live_keys)
    upper_small, upper_pairs, d_first = back_upper(gathered, saved, cotangent)
    lower_small, lower_pairs, input_grad = back_lower(gathered, saved, d_first)
    all_pairs = lower_pairs + upper_pairs
    all_sums = lax.psum_scatter(
        owner_terms(
            all_pairs,
            group_size,
            width,
            lax.axis_size("fsdp") * owner_rows(all_pairs, group_size, width),
        ),
        "fsdp",
        scatter_dimension=0,
        tiled=True,
    )
    large = unpack_rows(all_pairs, all_sums, group_size, width)
    small = (
        lax.psum_scatter(lower_small[0], "fsdp", scatter_dimension=0, tiled=True),
        lax.psum_scatter(lower_small[1], "fsdp", scatter_dimension=0, tiled=True),
        lax.psum_scatter(lower_small[2], "fsdp", scatter_dimension=0, tiled=True),
        lax.psum_scatter(upper_small[0], "fsdp", scatter_dimension=0, tiled=True),
        lax.psum_scatter(upper_small[1], "fsdp", scatter_dimension=0, tiled=True),
        lax.psum_scatter(upper_small[2], "fsdp", scatter_dimension=0, tiled=True),
        lax.psum_scatter(upper_small[3], "fsdp", scatter_dimension=0, tiled=True),
        lax.psum_scatter(upper_small[4], "fsdp", scatter_dimension=0, tiled=True),
        lax.psum_scatter(upper_small[5], "fsdp", scatter_dimension=0, tiled=True),
    )
    return (
        layer_out,
        input_grad,
        large[0],
        small[0],
        small[1],
        large[1],
        small[2],
        small[3],
        small[4],
        large[2],
        small[5],
        large[3],
        small[6],
        small[7],
        small[8],
    )


def solution(mesh):
    placed = (
        P("fsdp", None),
        P("fsdp"),
        P("fsdp", None),
        P("fsdp"),
        P("fsdp"),
        P("fsdp", None),
        P("fsdp"),
        P("fsdp"),
        P("fsdp"),
        P("fsdp", None),
        P("fsdp"),
        P("fsdp", None),
        P("fsdp"),
        P("fsdp"),
        P("fsdp"),
        P("fsdp", None),
    )
    return jax.shard_map(
        body,
        mesh=mesh,
        in_specs=placed,
        out_specs=(
            P("fsdp", None),
            P("fsdp", None),
            P("fsdp", None),
            P("fsdp"),
            P("fsdp"),
            P("fsdp", None),
            P("fsdp"),
            P("fsdp"),
            P("fsdp"),
            P("fsdp", None),
            P("fsdp"),
            P("fsdp", None),
            P("fsdp"),
            P("fsdp"),
            P("fsdp"),
        ),
        check_vma=False,
    )
```

profile of v0, /device:TPU:0, one launch (start us, length us, event | category | flops | bytes accessed | tf_op | source)
XLA Modules:
  0.0 865.7 jit_solution(8831968162804845587)
XLA Ops:
  7.2 0.7 all-gather.6.cloned.1.call-update
  8.0 0.7 all-gather.8.cloned.1.call-update
  8.7 0.7 all-gather.10.cloned.1.call-update
  10.0 0.8 dynamic-update-slice.7
  10.9 0.8 dynamic-update-slice.3
  11.7 0.8 dynamic-update-slice.4
  12.6 0.8 dynamic-update-slice.5
  13.4 0.8 dynamic-update-slice.2
  14.2 0.8 dynamic-update-slice.1
  15.1 0.8 dynamic-update-slice
  15.9 0.8 dynamic-update-slice.6
  16.7 43.4 %all-reduce.18 = (bf16[1024]{0:T(1024)(128)(2,1)S(1)}, bf16[1024]{0:T(1024)(128)(2,1)S(1)}, bf16[1024]{0:T(1024)(128)(2,1)S(1)}, bf16[1024]{0:T(1024)(128)(2,1)S...) all-reduce(bf16[1024]{0:T(1024)(128)(2,1)S(1)} %dynamic-update-slic, ...), channel_id=1, replica_groups=mesh['fsdp'=32] {'fsdp'}, use_global_device_ids=true, to_apply=%add | all-reduce | flops 8192 | bytes 32768
  60.2 39.8 %all-gather = bf16[32,1,128]{2,1,0:T(2,128)(2,1)S(1)} all-gather(bf16[1,1,128]{2,1,0:T(2,128)(2,1)} %bitcast.74), channel_id=1, replica_groups=mesh['fsdp'=32] {'fsdp'}, dimensions={0}, use_global_device_ids=true | all-gather | bytes 8448 | tf_op jit(solution)/shard_map/all_gather | solution.py:298
  100.0 0.7 broadcast_compare_fusion
  100.7 3.9 fusion.47
  105.8 0.8 copy-done.1
  107.0 33.6 %all-gather.8.cloned.1.call-done = bf16[1024,1024]{1,0:T(8,128)(2,1)} async-done(((bf16[32,1024]{1,0:T(8,128)(2,1)}), bf16[1024,1024]{1,0:T(8,128)(2,1)}) %all-gather.8.cloned.1.call-update) | async-done | bytes 2097168 | tf_op jit(solution)/shard_map/all_gather | solution.py:293
  140.6 2.1 fusion.44
  143.0 76.4 %all-gather.10.cloned.1.call-done = bf16[1024,4096]{1,0:T(8,128)(2,1)} async-done(((bf16[32,4096]{1,0:T(8,128)(2,1)}), bf16[1024,4096]{1,0:T(8,128)(2,1)}) %all-gather.10.cloned.1.call-update) | async-done | bytes 8388624 | tf_op jit(solution)/shard_map/all_gather | solution.py:297
  219.4 4.7 convolution_add_fusion
  224.1 73.7 %all-gather.12.cloned.1.call-done = bf16[4096,1024]{1,0:T(8,128)(2,1)} async-done(((bf16[128,1024]{1,0:T(8,128)(2,1)}), bf16[4096,1024]{1,0:T(8,128)(2,1)}) %all-gather.12.cloned.1.call-update) | async-done | bytes 8388624 | tf_op jit(solution)/shard_map/all_gather | solution.py:299
  297.8 5.0 fusion.45
  303.4 1.0 fusion.37
  304.3 3.4 fusion.46
  307.8 3.0 multiply_reduce_fusion.1
  311.1 0.8 copy-done.4
  311.9 1.5 convolution_convert_fusion.1
  313.5 1.8 copy.56
  315.3 1.9 fusion.41
  317.3 1.5 multiply_reduce_fusion
  320.1 8.1 fusion.30
  328.2 8.2 fusion.22
  336.4 2.6 fusion.26
  339.1 6.3 convolution_bitcast_fusion
  345.4 12.6 %copy.60 = f32[1024,3072]{1,0:T(8,128)} copy(f32[1024,3072]{0,1:T(8,128)} %convolution_bitcast_fusion) | data formatting | bytes 25165824 | tf_op jit(solution)/shard_map/tk,tw->kw/dot_general | solution.py:253
  358.0 14.1 %reshape.148 = f32[32,96,1024]{2,1,0:T(8,128)} reshape(f32[1024,3072]{1,0:T(8,128)} %copy.60) | data formatting | bytes 25165824 | tf_op jit(solution)/shard_map/reshape | solution.py:254
  372.2 19.1 %reshape.149 = f32[32,128,1024]{2,1,0:T(8,128)} reshape(f32[1024,4096]{1,0:T(8,128)} %fusion.22) | data formatting | bytes 33554432 | tf_op jit(solution)/shard_map/reshape | solution.py:254
  391.2 33.3 %pad_maximum_fusion = f32[32,384,1024]{2,1,0:T(8,128)} fusion(f32[32,128,1024]{2,1,0:T(8,128)} %bitcast.54, f32[32,128,1024]{2,1,0:T(8,128)} %reshape.149, f32[32,32,1024]{2,1,0:T(8,128)} %fusion.26, f32[32,96,1024]{2,1,0:T(8,128)} %reshape.148), kind=kLoop, calls=%fused_computation | loop fusion | flops 37748736 | bytes 100663296 | tf_op jit(solution)/shard_map/concatenate | solution.py:255
  424.7 40.0 %all-reduce.17 = (f32[1024]{0:T(1024)S(1)}, f32[1024]{0:T(1024)S(1)}, f32[1024]{0:T(1024)S(1)}, f32[1024]{0:T(1024)S(1)}, f32[1024]{0:T(1024)S(1)}, /*index=5*/f...) all-reduce(f32[1024]{0:T(1024)S(1)} %reduce_sum.186, ...), channel_id=3, replica_groups=mesh['fsdp'=32] {'fsdp'}, use_global_device_ids=true, to_apply=%region_13.14.clone | all-reduce | flops 12288 | bytes 98304
  464.7 0.6 dynamic-slice
  469.4 0.6 dynamic-slice.5
  470.0 7.0 fusion.7
  477.0 375.5 %reduce-scatter.2.cloned.1.call-done = f32[384,1024]{1,0:T(8,128)} async-done(((f32[12288,1024]{1,0:T(8,128)}), f32[384,1024]{1,0:T(8,128)}) %reduce-scatter.2.cloned.1.call-update) | async-done | bytes 1572880 | tf_op jit(solution)/shard_map/reduce_scatter | solution.py:308
  852.6 1.0 slice.32
  853.6 0.9 reshape.152
  854.5 2.1 fusion.40
  856.6 1.0 reshape.153
  857.6 1.6 slice.33
  (108 shorter events, 8.8 us)
Async XLA Ops:
  7.2 93.5 %all-gather.6.cloned.1.call-start = ((), (), s32[]{:S(2)}) async-start(), calls=%async_computation.1 | async-start | bytes 6488064 | tf_op jit(solution)/shard_map/all_gather | solution.py:290
  7.9 132.7 %all-gather.8.cloned.1.call-start = ((), (), s32[]{:S(2)}) async-start(), calls=%async_computation.2 | async-start | bytes 2162688 | tf_op jit(solution)/shard_map/all_gather | solution.py:293
  8.7 210.7 %all-gather.10.cloned.1.call-start = ((), (), s32[]{:S(2)}) async-start(), calls=%async_computation.3 | async-start | bytes 8650752 | tf_op jit(solution)/shard_map/all_gather | solution.py:297
  9.4 288.4 %all-gather.12.cloned.1.call-start = ((), (), s32[]{:S(2)}) async-start(), calls=%async_computation.4 | async-start | bytes 8650752 | tf_op jit(solution)/shard_map/all_gather | solution.py:299
  10.0 842.6 %reduce-scatter.2.cloned.1.call-start = ((), (), s32[]{:S(2)}) async-start(), calls=%async_computation.5 | async-start | bytes 51904512 | tf_op jit(solution)/shard_map/reduce_scatter | solution.py:308
  104.9 2.0 copy-start.11
  105.1 1.9 copy-start.9
  105.3 1.7 copy-start.21
  105.7 1.0 copy-start.1
  106.6 34.0 %copy-start.8 = (bf16[128,1024]{1,0:T(8,128)(2,1)S(1)}, bf16[128,1024]{1,0:T(8,128)(2,1)}, u32[]{:S(2)}) copy-start(bf16[128,1024]{1,0:T(8,128)(2,1)} %param.16) | copy-start | bytes 786436
  107.0 112.4 %copy-start.22 = (bf16[16,64,128]{2,1,0:T(8,128)(2,1)}, bf16[16,64,128]{2,1,0:T(8,128)(2,1)S(1)}, u32[]{:S(2)}) copy-start(bf16[16,64,128]{2,1,0:T(8,128)(2,1)S(1)} %convolution_convert_fusion.2) | copy-start | bytes 786436
  224.1 78.9 %copy-start.19 = (bf16[128,1024]{1,0:T(8,128)(2,1)S(1)}, bf16[128,1024]{1,0:T(8,128)(2,1)}, u32[]{:S(2)}) copy-start(bf16[128,1024]{1,0:T(8,128)(2,1)} %param.31) | copy-start | bytes 786436
  297.8 5.5 copy-start.20
  297.8 6.5 copy-start
  303.4 4.4 slice-start
  304.3 3.5 slice-start.1
  307.8 3.1 copy-start.6
  307.8 4.1 copy-start.3
  311.1 0.8 copy-start.4
  315.3 2.0 copy-start.2
  317.2 21.8 %copy-start.13 = (bf16[128,16,64]{0,2,1:T(8,128)(2,1)}, bf16[128,16,64]{0,2,1:T(8,128)(2,1)S(1)}, u32[]{:S(2)}) copy-start(bf16[128,16,64]{0,2,1:T(8,128)(2,1)S(1)} %get-tuple-element.50) | copy-start | bytes 786436
  317.2 1.8 copy-start.12
  318.8 1.0 copy-start.10
  319.7 19.3 %copy-start.15 = (bf16[16,64,128]{2,1,0:T(8,128)(2,1)}, bf16[16,64,128]{2,1,0:T(8,128)(2,1)S(1)}, u32[]{:S(2)}) copy-start(bf16[16,64,128]{2,1,0:T(8,128)(2,1)S(1)} %convolution_convert_fusion) | copy-start | bytes 786436
  320.1 19.0 %copy-start.17 = (bf16[128,16,64]{0,2,1:T(8,128)(2,1)}, bf16[128,16,64]{0,2,1:T(8,128)(2,1)S(1)}, u32[]{:S(2)}) copy-start(bf16[128,16,64]{0,2,1:T(8,128)(2,1)S(1)} %get-tuple-element.52) | copy-start | bytes 786436
  320.1 8.1 copy-start.7
  328.2 8.2 copy-start.5
  328.2 8.2 copy-start.23
  424.6 45.4 %copy-start.14 = (bf16[128,16,64]{0,2,1:T(8,128)(2,1)S(1)}, bf16[128,16,64]{0,2,1:T(8,128)(2,1)}, u32[]{:S(2)}) copy-start(bf16[128,16,64]{0,2,1:T(8,128)(2,1)} %copy-done.13) | copy-start | bytes 786436
  424.6 45.4 %copy-start.16 = (bf16[16,64,128]{2,1,0:T(8,128)(2,1)S(1)}, bf16[16,64,128]{2,1,0:T(8,128)(2,1)}, u32[]{:S(2)}) copy-start(bf16[16,64,128]{2,1,0:T(8,128)(2,1)} %copy-done.15) | copy-start | bytes 786436
  424.6 45.4 %copy-start.18 = (bf16[128,16,64]{0,2,1:T(8,128)(2,1)S(1)}, bf16[128,16,64]{0,2,1:T(8,128)(2,1)}, u32[]{:S(2)}) copy-start(bf16[128,16,64]{0,2,1:T(8,128)(2,1)} %copy-done.17) | copy-start | bytes 786436
Sparse Core Ops, SparseCore 0:
  10.8 72.0 all-gather.5
  85.8 54.7 all-gather.7
  143.5 75.8 all-gather.9
  222.1 75.6 all-gather.11
  424.7 427.7 reduce-scatter.1
where the time goes:
time: 867 us; the launch traced here: 866 us
  waiting for transfers between devices  562 us (65%)
  blocking collectives  123 us (14%)
  local copies, waits for them, and re-layouts  68.7 us (8%)
  matrix products  61 us (7%)
  other arithmetic  36.5 us (4%)
  between operations  14.3 us (2%)
    reduce_scatter x1, waiting for transfers between devices, body(): lax.psum_scatter(owner_terms(all_pairs, group_size, width, lax.axis_size(...  376 us
    unnamed x2, blocking collectives  83.4 us
    all_gather x1, waiting for transfers between devices, body(): lax.all_gather(expand_weight, 'fsdp', axis=0, tiled=True)  76.4 us
    all_gather x1, waiting for transfers between devices, body(): lax.all_gather(shrink_weight, 'fsdp', axis=0, tiled=True)  73.7 us
    all_gather x1, blocking collectives, body(): lax.all_gather(expand_bias, 'fsdp', axis=0, tiled=True)  39.8 us
    all_gather x1, waiting for transfers between devices, body(): lax.all_gather(output_weight, 'fsdp', axis=0, tiled=True)  33.6 us
    concatenate x1, other arithmetic, owner_terms(): return jnp.concatenate(pieces, axis=1).reshape(owners * per_owner, width)  33.3 us
    reshape x2, local copies, waits for them, and re-layouts, owner_terms(): pieces.append(term.reshape(owners, share * right.shape[1] // width, width))  33.2 us
  transfers between devices with their start and end apart: 5, of which 4 were waited for; matrix products, arithmetic and copies ran while one was open for 4% of the time, Pallas kernels for 0%

commit v1 on v0

--- a/solution.py
+++ b/solution.py
@@ -240,30 +240,84 @@
     return (small, pairs, input_grad)
 
 
-def owner_rows(pairs, group_size, width):
-    return sum((left.shape[1] // group_size * right.shape[1] // width for left, right in pairs))
-
-
-def owner_terms(pairs, group_size, width, count):
-    per_owner = owner_rows(pairs, group_size, width)
-    owners = count // per_owner
-    pieces = []
-    for left, right in pairs:
-        share = left.shape[1] // group_size
-        term = jnp.einsum("tk,tw->kw", left, right, preferred_element_type=jnp.float32)
-        pieces.append(term.reshape(owners, share * right.shape[1] // width, width))
-    return jnp.concatenate(pieces, axis=1).reshape(owners * per_owner, width)
-
-
-def unpack_rows(pairs, summed, group_size, width):
+def swap(value, bit, count):
+    return lax.ppermute(value, "fsdp", [(i, i ^ (1 << bit)) for i in range(count)])
+
+
+def own_bit(bit):
+    return (lax.axis_index("fsdp") >> bit) & 1
+
+
+def join(own, other, bit, levels):
+    first = own_bit(bit) == 0
+    return jnp.concatenate(
+        [jnp.where(first, own, other), jnp.where(first, other, own)], axis=levels - 1 - bit
+    )
+
+
+def orders(levels):
+    ring = list(range(1, levels))
+    return [ring[k * len(ring) // 3 :] + ring[: k * len(ring) // 3] for k in range(3)]
+
+
+def collect(shard, order, count):
+    levels = count.bit_length() - 1
+    held = shard.reshape((1,) * levels + shard.shape)
+    steps = list(reversed(order))
+    for bit in steps[:-1]:
+        held = join(held, swap(held, bit, count), bit, levels)
+    bit = steps[-1]
+    across = swap(held, bit, count)
+    beside = swap(held, 0, count)
+    corner = swap(across, 0, count)
+    held = join(join(held, across, bit, levels), join(beside, corner, bit, levels), 0, levels)
+    return held.reshape((count * shard.shape[0],) + shard.shape[1:])
+
+
+def halve(terms, order, count, last):
+    levels = count.bit_length() - 1
+    for bit in order:
+        axis = terms.ndim - 3 - bit if last else terms.ndim - 2 - bit
+        mine = own_bit(bit)
+        keep = lax.dynamic_slice_in_dim(terms, mine, 1, axis)
+        send = lax.dynamic_slice_in_dim(terms, 1 - mine, 1, axis)
+        total = keep.astype(jnp.float32) + swap(send, bit, count).astype(jnp.float32)
+        terms = total if bit == order[-1] else total.astype(terms.dtype)
+    return terms.reshape(terms.shape[-2:])
+
+
+def by_core(left, count):
+    parts = left.reshape(left.shape[0], count // 2, 2, left.shape[1] // count)
+    core = own_bit(0)
+    pick = lambda at: lax.dynamic_index_in_dim(parts, at, 2, keepdims=False).reshape(
+        left.shape[0], left.shape[1] // 2
+    )
+    return (pick(core), pick(1 - core))
+
+
+def pair_up(left, right, count):
+    mine, other = by_core(left, count)
+    return (
+        jnp.concatenate([mine, swap(other, 0, count)], axis=0),
+        jnp.concatenate([right, swap(right, 0, count)], axis=0),
+    )
+
+
+def summed_grad(left, right, pieces, count):
+    levels = count.bit_length() - 1
     results = []
     offset = 0
-    for left, right in pairs:
-        share = left.shape[1] // group_size
-        extent = share * right.shape[1] // width
-        results.append(summed[offset : offset + extent].reshape(share, right.shape[1]))
+    for extent, order in pieces:
+        term = jnp.einsum(
+            "tk,tw->kw",
+            left,
+            right[:, offset : offset + extent],
+            preferred_element_type=jnp.float32,
+        ).astype(jnp.bfloat16)
+        term = term.reshape((2,) * (levels - 1) + (left.shape[1] * 2 // count, extent))
+        results.append(halve(term, order, count, False))
         offset = offset + extent
-    return tuple(results)
+    return results[0] if len(results) == 1 else jnp.concatenate(results, axis=1)
 
 
 def body(
@@ -284,63 +338,85 @@
     second_shift,
     cotangent,
 ):
-    group_size = lax.axis_size("fsdp")
+    count = lax.axis_size("fsdp")
+    levels = count.bit_length() - 1
     width = inputs.shape[1]
+    ways = orders(levels)
+    vectors = (
+        query_bias,
+        value_bias,
+        output_bias,
+        first_gain,
+        first_shift,
+        expand_bias,
+        shrink_bias,
+        second_gain,
+        second_shift,
+    )
+    packed = collect(jnp.concatenate(vectors)[None, :], ways[0], count)
+    wide = []
+    offset = 0
+    for vector in vectors:
+        wide.append(packed[:, offset : offset + vector.shape[0]].reshape(-1))
+        offset = offset + vector.shape[0]
     gathered = (
-        lax.all_gather(triple_weight, "fsdp", axis=0, tiled=True),
-        lax.all_gather(query_bias, "fsdp", axis=0, tiled=True),
-        lax.all_gather(value_bias, "fsdp", axis=0, tiled=True),
-        lax.all_gather(output_weight, "fsdp", axis=0, tiled=True),
-        lax.all_gather(output_bias, "fsdp", axis=0, tiled=True),
-        lax.all_gather(first_gain, "fsdp", axis=0, tiled=True),
-        lax.all_gather(first_shift, "fsdp", axis=0, tiled=True),
-        lax.all_gather(expand_weight, "fsdp", axis=0, tiled=True),
-        lax.all_gather(expand_bias, "fsdp", axis=0, tiled=True),
-        lax.all_gather(shrink_weight, "fsdp", axis=0, tiled=True),
-        lax.all_gather(shrink_bias, "fsdp", axis=0, tiled=True),
-        lax.all_gather(second_gain, "fsdp", axis=0, tiled=True),
-        lax.all_gather(second_shift, "fsdp", axis=0, tiled=True),
+        collect(triple_weight, ways[2], count),
+        wide[0],
+        wide[1],
+        collect(output_weight, ways[0], count),
+        wide[2],
+        wide[3],
+        wide[4],
+        collect(expand_weight, ways[0], count),
+        wide[5],
+        collect(shrink_weight, ways[1], count),
+        wide[6],
+        wide[7],
+        wide[8],
     )
     layer_out, saved = forward(gathered, inputs, live_keys)
     upper_small, upper_pairs, d_first = back_upper(gathered, saved, cotangent)
     lower_small, lower_pairs, input_grad = back_lower(gathered, saved, d_first)
-    all_pairs = lower_pairs + upper_pairs
-    all_sums = lax.psum_scatter(
-        owner_terms(
-            all_pairs,
-            group_size,
-            width,
-            lax.axis_size("fsdp") * owner_rows(all_pairs, group_size, width),
-        ),
-        "fsdp",
-        scatter_dimension=0,
-        tiled=True,
-    )
-    large = unpack_rows(all_pairs, all_sums, group_size, width)
-    small = (
-        lax.psum_scatter(lower_small[0], "fsdp", scatter_dimension=0, tiled=True),
-        lax.psum_scatter(lower_small[1], "fsdp", scatter_dimension=0, tiled=True),
-        lax.psum_scatter(lower_small[2], "fsdp", scatter_dimension=0, tiled=True),
-        lax.psum_scatter(upper_small[0], "fsdp", scatter_dimension=0, tiled=True),
-        lax.psum_scatter(upper_small[1], "fsdp", scatter_dimension=0, tiled=True),
-        lax.psum_scatter(upper_small[2], "fsdp", scatter_dimension=0, tiled=True),
-        lax.psum_scatter(upper_small[3], "fsdp", scatter_dimension=0, tiled=True),
-        lax.psum_scatter(upper_small[4], "fsdp", scatter_dimension=0, tiled=True),
-        lax.psum_scatter(upper_small[5], "fsdp", scatter_dimension=0, tiled=True),
-    )
+    hidden = expand_weight.shape[1]
+    shrink_grad = summed_grad(
+        *pair_up(*upper_pairs[1], count),
+        ((width * 3 // 4, ways[1]), (width // 4, ways[2])),
+        count,
+    )
+    expand_grad = summed_grad(
+        *pair_up(*upper_pairs[0], count),
+        ((hidden * 3 // 4, ways[0]), (hidden // 4, ways[2])),
+        count,
+    )
+    output_grad = summed_grad(*pair_up(*lower_pairs[1], count), ((width, ways[1]),), count)
+    triple_grad = summed_grad(
+        *pair_up(*lower_pairs[0], count),
+        ((width, ways[0]), (width, ways[1]), (width, ways[2])),
+        count,
+    )
+    sums = lower_small + upper_small
+    terms = jnp.concatenate([item.reshape(count, -1) for item in sums], axis=1)
+    terms = terms.reshape((2,) * levels + (1, terms.shape[1]))
+    owned = halve(terms, list(range(levels)), count, True)[0]
+    small = []
+    offset = 0
+    for item in sums:
+        extent = item.shape[0] // count
+        small.append(owned[offset : offset + extent])
+        offset = offset + extent
     return (
         layer_out,
         input_grad,
-        large[0],
+        triple_grad,
         small[0],
         small[1],
-        large[1],
+        output_grad,
         small[2],
         small[3],
         small[4],
-        large[2],
+        expand_grad,
         small[5],
-        large[3],
+        shrink_grad,
         small[6],
         small[7],
         small[8],

time: 867 us -> 441 us (0.51)
  waiting for transfers between devices: 562 us -> 207 us
  blocking collectives: 123 us -> 0 us
  starting transfers between devices: 0.19 us -> 80.2 us
  local copies, waits for them, and re-layouts: 68.7 us -> 33.5 us
  other arithmetic: 36.5 us -> 67.7 us
  matrix products: 61 us -> 43.3 us
  between operations: 14.3 us -> 2.9 us
    reduce_scatter x1 -> x0, waiting for transfers between devices: 376 us -> none  [body(): lax.psum_scatter(owner_terms(all_pairs, group_size, width, lax.axis_size(...]
    ppermute x0 -> x75, waiting for transfers between devices: none -> 207 us  [swap(): lax.ppermute(value, 'fsdp', [(i, i ^ 1 << bit) for i in range(count)])]
    all_gather x4 -> x0, waiting for transfers between devices: 184 us -> none  [the longest x1 76.4 us: body(): lax.all_gather(expand_weight, 'fsdp', axis=0, tiled=True)]
    unnamed x2 -> x0, blocking collectives: 83.4 us -> none
    ppermute x0 -> x75, starting transfers between devices: none -> 80.2 us  [swap(): lax.ppermute(value, 'fsdp', [(i, i ^ 1 << bit) for i in range(count)])]
    all_gather x1 -> x0, blocking collectives: 39.8 us -> none  [body(): lax.all_gather(expand_bias, 'fsdp', axis=0, tiled=True)]
    reshape x4 -> x2, local copies, waits for them, and re-layouts: 35.1 us -> 0.77 us  [the longest x1 0.75 us: by_core(): parts = left.reshape(left.shape[0], count // 2, 2, left.shape[1] // count)]
    select_n x0 -> x30, other arithmetic: none -> 27.7 us  [join(): jnp.where(first, own, other)]
  transfers between devices with their start and end apart: 5 -> 75, of which waited for: 4 -> 28; matrix products, arithmetic and copies ran while one was open for 4% -> 30% of each run, Pallas kernels for 0% -> 0%
where the time goes in v1:
time: 441 us; the launch traced here: 435 us
  waiting for transfers between devices  207 us (47%)
  starting transfers between devices  80.2 us (18%)
  other arithmetic  67.7 us (15%)
  matrix products  43.3 us (10%)
  local copies, waits for them, and re-layouts  33.5 us (8%)
    ppermute x75, waiting for transfers between devices, swap(): lax.ppermute(value, 'fsdp', [(i, i ^ 1 << bit) for i in range(count)])  207 us
    ppermute x75, starting transfers between devices, swap(): lax.ppermute(value, 'fsdp', [(i, i ^ 1 << bit) for i in range(count)])  80.2 us
    select_n x30, other arithmetic, join(): jnp.where(first, own, other)  27.7 us
    concatenate x20, other arithmetic, join(): jnp.concatenate([jnp.where(first, own, other), jnp.where(first, other, ow...  22.1 us
    dot_general x8, matrix products, summed_grad(): jnp.einsum('tk,tw->kw', left, right[:, offset:offset + extent], preferred...  12.2 us
    unnamed x143, local copies, waits for them, and re-layouts  9.48 us
  transfers between devices with their start and end apart: 75, of which 28 were waited for; matrix products, arithmetic and copies ran while one was open for 30% of the time, Pallas kernels for 0%

profile of v1, /device:TPU:0, one launch (start us, length us, event | category | flops | bytes accessed | tf_op | source)
XLA Modules:
  0.0 435.0 jit_solution(14375695726973179361)
XLA Ops:
  0.7 6.1 %concatenate.318 = bf16[384]{0:T(512)(128)(2,1)S(1)} concatenate(bf16[32]{0:T(256)(128)(2,1)} %param.19, bf16[32]{0:T(256)(128)(2,1)} %param.20, bf16[32]{0:T(256)(128)(2,1)} %param.22, bf16[32]{0:T(256)(128)(2,1)} %param.23, bf16[32]{0:T(256)(128)(2,1)} %param.24, bf16[128]{0:T(256)(128)(2,1)} %param.26, bf16[32]{0:T(256)(128)(2,1)} %param.28, bf16[32]{0:T(256)(128)(2,1)} %param.29, ...), dimensions={0} | concatenate | bytes 1536 | tf_op jit(solution)/shard_map/concatenate | solution.py:356
  6.8 4.1 collective-permute-start.6
  14.5 2.6 collective-permute-start.12
  25.3 2.3 collective-permute-done.9
  31.1 6.2 %collective-permute-done.13 = bf16[2,1,1,1,1,32,1024]{6,5,4,3,2,1,0:T(8,128)(2,1)S(1)} collective-permute-done((bf16[2,1,1,1,1,32,1024]{6,5,4,3,2,1,0:T(8,128)(2,1)S(1)}, bf16[2,1,1,1,1,32,1024]{6,5,4,3,2,1,0:T(8,128)(2,1)S(1)}, u32[]{:S(2)}, u32[]{:S(2)}) %collective-permute-start.13) | collective-permute-done | bytes 131104 | tf_op jit(solution)/shard_map/ppermute | solution.py:244
  40.0 3.6 collective-permute-start.25
  48.9 3.6 collective-permute-start.2
  52.5 16.5 %collective-permute-done.25 = bf16[1,1,1,2,1,128,1024]{6,5,4,3,2,1,0:T(8,128)(2,1)S(1)} collective-permute-done((bf16[1,1,1,2,1,128,1024]{6,5,4,3,2,1,0:T(8,128)(2,1)S(1)}, bf16[1,1,1,2,1,128,1024]{6,5,4,3,2,1,0:T(8,128)(2,1)S(1)}, u32[]{:S(2)}, u32[]{:S(2)}) %collective-permute-start.25) | collective-permute-done | bytes 524320 | tf_op jit(solution)/shard_map/ppermute | solution.py:244
  70.1 29.8 %collective-permute-done.2 = bf16[1,1,2,2,1,32,3072]{6,5,4,3,2,1,0:T(8,128)(2,1)S(1)} collective-permute-done((bf16[1,1,2,2,1,32,3072]{6,5,4,3,2,1,0:T(8,128)(2,1)S(1)}, bf16[1,1,2,2,1,32,3072]{6,5,4,3,2,1,0:T(8,128)(2,1)S(1)}, u32[]{:S(2)}, u32[]{:S(2)}) %collective-permute-start.2) | collective-permute-done | bytes 786464 | tf_op jit(solution)/shard_map/ppermute | solution.py:244
  101.6 8.5 %collective-permute-done.26 = bf16[2,1,1,2,1,128,1024]{6,5,4,3,2,1,0:T(8,128)(2,1)S(1)} collective-permute-done((bf16[2,1,1,2,1,128,1024]{6,5,4,3,2,1,0:T(8,128)(2,1)S(1)}, bf16[2,1,1,2,1,128,1024]{6,5,4,3,2,1,0:T(8,128)(2,1)S(1)}, u32[]{:S(2)}, u32[]{:S(2)}) %collective-permute-start.26) | collective-permute-done | bytes 1048608 | tf_op jit(solution)/shard_map/ppermute | solution.py:244
  124.4 16.0 %collective-permute-done.3 = bf16[2,1,2,2,1,32,3072]{6,5,4,3,2,1,0:T(8,128)(2,1)} collective-permute-done((bf16[2,1,2,2,1,32,3072]{6,5,4,3,2,1,0:T(8,128)(2,1)}, bf16[2,1,2,2,1,32,3072]{6,5,4,3,2,1,0:T(8,128)(2,1)}, u32[]{:S(2)}, u32[]{:S(2)}) %collective-permute-start.3) | collective-permute-done | bytes 1572896 | tf_op jit(solution)/shard_map/ppermute | solution.py:244
  142.1 10.6 %collective-permute-done.27 = bf16[2,2,1,2,1,128,1024]{6,5,4,3,2,1,0:T(8,128)(2,1)} collective-permute-done((bf16[2,2,1,2,1,128,1024]{6,5,4,3,2,1,0:T(8,128)(2,1)}, bf16[2,2,1,2,1,128,1024]{6,5,4,3,2,1,0:T(8,128)(2,1)}, u32[]{:S(2)}, u32[]{:S(2)}) %collective-permute-start.27) | collective-permute-done | bytes 2097184 | tf_op jit(solution)/shard_map/ppermute | solution.py:244
  152.7 4.0 broadcast_select_fusion.9
  157.2 4.1 broadcast_select_fusion.13
  171.4 2.6 broadcast_select_fusion.7
  174.8 3.7 broadcast_select_fusion.1
  178.5 7.6 %pad_maximum_fusion.1 = bf16[2,2,2,2,2,128,1024]{6,5,4,3,2,1,0:T(8,128)(2,1)} fusion(bf16[2,2,2,2,1,128,1024]{6,5,4,3,2,1,0:T(8,128)(2,1)} %get-tuple-element.28, bf16[2,2,2,2,1,128,1024]{6,5,4,3,2,1,0:T(8,128)(2,1)} %get-tuple-element.27), kind=kLoop, calls=%fused_computation.1 | loop fusion | flops 4194304 | bytes 16777216 | tf_op jit(solution)/shard_map/concatenate | solution.py:253
  186.1 2.6 broadcast_select_fusion.11
  189.6 3.6 broadcast_select_fusion.3
  193.2 7.6 %pad_maximum_fusion = bf16[2,2,2,2,2,32,4096]{6,5,4,3,2,1,0:T(8,128)(2,1)} fusion(bf16[2,2,2,2,1,32,4096]{6,5,4,3,2,1,0:T(8,128)(2,1)} %get-tuple-element.30, bf16[2,2,2,2,1,32,4096]{6,5,4,3,2,1,0:T(8,128)(2,1)} %get-tuple-element.29), kind=kLoop, calls=%fused_computation | loop fusion | flops 4194304 | bytes 16777216 | tf_op jit(solution)/shard_map/concatenate | solution.py:253
  200.8 4.4 %multiply_convert_fusion = (bf16[128,4096]{1,0:T(8,128)(2,1)S(1)}, f32[128,4096]{1,0:T(8,128)S(1)}) fusion(f32[4096]{0:T(1024)S(1)} %copy-done.42, bf16[128,1024]{1,0:T(8,128)(2,1)S(1)} %fusion.31, bf16[1024,4096]{1,0:T(8,128)(2,1)} %bitcast.121), kind=kOutput, calls=%fused_computation.33 | convolution fusion | flops 1076887552 | bytes 11812864 | tf_op jit(solution)/shard_map/dot_general | solution.py:91
  205.3 5.2 %fusion.59 = (f32[128]{0:T(128)S(1)}, f32[128,1024]{1,0:T(8,128)S(1)}) fusion(f32[1024]{0:T(1024)S(1)} %copy-done.60, bf16[128,4096]{1,0:T(8,128)(2,1)S(1)} %get-tuple-element.124, bf16[4096,1024]{1,0:T(8,128)(2,1)} %bitcast.125, f32[1024]{0:T(1024)S(1)} %reshape.906, f32[1024]{0:T(1024)S(1)} %reshape.905, f32[128]{0:T(128)S(1)} %copy-done.64, ...), kind=kOutput, calls=%fused_computation.314 | convolution fusion | flops 1074659200 | bytes 10499584 | tf_op jit(solution)/shard_map/dot_general | solution.py:97
  213.9 5.6 %fusion.54 = (f32[4096]{0:T(1024)}, bf16[128,4096]{1,0:T(8,128)(2,1)S(1)}) fusion(f32[128,4096]{1,0:T(8,128)S(1)} %get-tuple-element.125, bf16[128,1024]{1,0:T(8,128)(2,1)} %convert_element_type.461, bf16[4096,1024]{1,0:T(8,128)(2,1)S(1)} %bitcast.128), kind=kOutput, calls=%fused_computation.309 | convolution fusion | flops 1079504896 | bytes 11812864 | tf_op jit(solution)/shard_map/dot_general | solution.py:157
  219.5 3.6 multiply_reduce_fusion.1
  238.3 2.7 collective-permute-done.45
  241.6 5.7 %fusion.9 = bf16[128,1024]{1,0:T(8,128)(2,1)} fusion(f32[128,1024]{1,0:T(8,128)S(1)} %copy-done.31, bf16[1024,3072]{1,0:T(8,128)(2,1)} %bitcast.130, bf16[128,1024]{0,1:T(8,128)(2,1)S(1)} %bitcast.147, bf16[128,1024]{0,1:T(8,128)(2,1)S(1)} %bitcast.153, bf16[128,1024]{0,1:T(8,128)(2,1)S(1)} %bitcast.150), kind=kOutput, calls=%fused_computation.67 | convolution fusion | flops 807927808 | bytes 7864320 | tf_op jit(solution)/shard_map/dot_general | solution.py:236
  247.4 2.6 collective-permute-start.47
  253.5 2.2 constant_dynamic-slice_fusion.9
  268.7 7.9 %collective-permute-done.51 = bf16[2,2,1,2,32,1024]{5,4,3,2,1,0:T(8,128)(2,1)S(1)} collective-permute-done((bf16[2,2,1,2,32,1024]{5,4,3,2,1,0:T(8,128)(2,1)S(1)}, bf16[2,2,1,2,32,1024]{5,4,3,2,1,0:T(8,128)(2,1)S(1)}, u32[]{:S(2)}, u32[]{:S(2)}) %collective-permute-start.51) | collective-permute-done | bytes 524320 | tf_op jit(solution)/shard_map/ppermute | solution.py:244
  291.9 6.9 %collective-permute-done.53 = bf16[1,1,1,2,32,1024]{5,4,3,2,1,0:T(8,128)(2,1)S(1)} collective-permute-done((bf16[1,1,1,2,32,1024]{5,4,3,2,1,0:T(8,128)(2,1)S(1)}, bf16[1,1,1,2,32,1024]{5,4,3,2,1,0:T(8,128)(2,1)S(1)}, u32[]{:S(2)}, u32[]{:S(2)}) %collective-permute-start.53) | collective-permute-done | bytes 131104 | tf_op jit(solution)/shard_map/ppermute | solution.py:244
  299.5 3.7 collective-permute-done.54
  303.3 3.4 collective-permute-start.72
  307.6 9.3 %collective-permute-done.72 = bf16[1,1,2,2,128,256]{5,4,3,2,1,0:T(8,128)(2,1)S(1)} collective-permute-done((bf16[1,1,2,2,128,256]{5,4,3,2,1,0:T(8,128)(2,1)S(1)}, bf16[1,1,2,2,128,256]{5,4,3,2,1,0:T(8,128)(2,1)S(1)}, u32[]{:S(2)}, u32[]{:S(2)}) %collective-permute-start.72) | collective-permute-done | bytes 262176 | tf_op jit(solution)/shard_map/ppermute | solution.py:244
  319.4 4.0 collective-permute-done.36
  325.1 26.9 %collective-permute-done.73 = bf16[1,1,2,1,128,256]{5,4,3,2,1,0:T(8,128)(2,1)S(1)} collective-permute-done((bf16[1,1,2,1,128,256]{5,4,3,2,1,0:T(8,128)(2,1)S(1)}, bf16[1,1,2,1,128,256]{5,4,3,2,1,0:T(8,128)(2,1)S(1)}, u32[]{:S(2)}, u32[]{:S(2)}) %collective-permute-start.73) | collective-permute-done | bytes 131104 | tf_op jit(solution)/shard_map/ppermute | solution.py:244
  352.7 4.1 collective-permute-done.74
  357.3 2.8 collective-permute-start.37
  360.3 3.5 collective-permute-start.62
  365.4 5.7 %collective-permute-done.37 = bf16[2,1,1,2,32,1024]{5,4,3,2,1,0:T(8,128)(2,1)S(1)} collective-permute-done((bf16[2,1,1,2,32,1024]{5,4,3,2,1,0:T(8,128)(2,1)S(1)}, bf16[2,1,1,2,32,1024]{5,4,3,2,1,0:T(8,128)(2,1)S(1)}, u32[]{:S(2)}, u32[]{:S(2)}) %collective-permute-start.37) | collective-permute-done | bytes 262176 | tf_op jit(solution)/shard_map/ppermute | solution.py:244
  371.2 4.0 collective-permute-start.38
  377.7 3.2 collective-permute-done.38
  382.6 3.5 collective-permute-done.35
  393.8 12.9 %collective-permute-done.68 = bf16[2,1,1,2,128,768]{5,4,3,2,1,0:T(8,128)(2,1)S(1)} collective-permute-done((bf16[2,1,1,2,128,768]{5,4,3,2,1,0:T(8,128)(2,1)S(1)}, bf16[2,1,1,2,128,768]{5,4,3,2,1,0:T(8,128)(2,1)S(1)}, u32[]{:S(2)}, u32[]{:S(2)}) %collective-permute-start.68) | collective-permute-done | bytes 786464 | tf_op jit(solution)/shard_map/ppermute | solution.py:244
  407.0 2.9 collective-permute-start.69
  410.2 2.7 collective-permute-start.59
  412.9 11.2 %collective-permute-done.69 = bf16[1,1,1,2,128,768]{5,4,3,2,1,0:T(8,128)(2,1)S(1)} collective-permute-done((bf16[1,1,1,2,128,768]{5,4,3,2,1,0:T(8,128)(2,1)S(1)}, bf16[1,1,1,2,128,768]{5,4,3,2,1,0:T(8,128)(2,1)S(1)}, u32[]{:S(2)}, u32[]{:S(2)}) %collective-permute-start.69) | collective-permute-done | bytes 393248 | tf_op jit(solution)/shard_map/ppermute | solution.py:244
  425.0 5.0 %collective-permute-done.70 = bf16[1,1,1,1,128,768]{5,4,3,2,1,0:T(8,128)(2,1)S(1)} collective-permute-done((bf16[1,1,1,1,128,768]{5,4,3,2,1,0:T(8,128)(2,1)S(1)}, bf16[1,1,1,1,128,768]{5,4,3,2,1,0:T(8,128)(2,1)S(1)}, u32[]{:S(2)}, u32[]{:S(2)}) %collective-permute-start.70) | collective-permute-done | bytes 196640 | tf_op jit(solution)/shard_map/ppermute | solution.py:244
  430.9 2.8 collective-permute-done.60
  (449 shorter events, 127.9 us)
Async XLA Ops:
  14.5 14.6 %collective-permute-start.12 = (bf16[1,1,1,1,1,32,1024]{6,5,4,3,2,1,0:T(8,128)(2,1)}, bf16[1,1,1,1,1,32,1024]{6,5,4,3,2,1,0:T(8,128)(2,1)S(1)}, u32[]{:S(2)}, u32[]{:S(2)}) collective-permute-start(bf16[1,1,1,1,1,32,1024]{6,5,4,3,2,1,0:T(8,128)(2,1)} %bitcast.181), channel_id=1, source_target_pairs={{0,16},{1,17},{2,18},{3,19},{4,20},{5,21},{6,22},{7,23},{8,24},{9,... | collective-permute-start | bytes 196616 | tf_op jit(solution)/shard_map/ppermute | solution.py:244
  17.1 21.2 %collective-permute-start = (bf16[1,1,1,1,1,32,3072]{6,5,4,3,2,1,0:T(8,128)(2,1)}, bf16[1,1,1,1,1,32,3072]{6,5,4,3,2,1,0:T(8,128)(2,1)S(1)}, u32[]{:S(2)}, u32[]{:S(2)}) collective-permute-start(bf16[1,1,1,1,1,32,3072]{6,5,4,3,2,1,0:T(8,128)(2,1)} %bitcast.179), channel_id=1, source_target_pairs={{0,4},{1,5},{2,6},{3,7},{4,0},{5,1},{6,2},{7,3},{8,12},{9,13},{10,... | collective-permute-start | bytes 589832 | tf_op jit(solution)/shard_map/ppermute | solution.py:244
  18.6 21.3 %collective-permute-start.24 = (bf16[1,1,1,1,1,128,1024]{6,5,4,3,2,1,0:T(8,128)(2,1)}, bf16[1,1,1,1,1,128,1024]{6,5,4,3,2,1,0:T(8,128)(2,1)S(1)}, u32[]{:S(2)}, u32[]{:S(2)}) collective-permute-start(bf16[1,1,1,1,1,128,1024]{6,5,4,3,2,1,0:T(8,128)(2,1)} %bitcast.177), channel_id=1, source_target_pairs={{0,2},{1,3},{2,0},{3,1},{4,6},{5,7},{6,4},{7,5},{8,10},{9,11},{10,... | collective-permute-start | bytes 786440 | tf_op jit(solution)/shard_map/ppermute | solution.py:244
  27.7 15.9 %collective-permute-start.18 = (bf16[1,1,1,1,1,32,4096]{6,5,4,3,2,1,0:T(8,128)(2,1)}, bf16[1,1,1,1,1,32,4096]{6,5,4,3,2,1,0:T(8,128)(2,1)S(1)}, u32[]{:S(2)}, u32[]{:S(2)}) collective-permute-start(bf16[1,1,1,1,1,32,4096]{6,5,4,3,2,1,0:T(8,128)(2,1)} %bitcast.178), channel_id=1, source_target_pairs={{0,16},{1,17},{2,18},{3,19},{4,20},{5,21},{6,22},{7,23},{8,24},{9,... | collective-permute-start | bytes 786440 | tf_op jit(solution)/shard_map/ppermute | solution.py:244
  38.3 10.5 %collective-permute-start.1 = (bf16[1,1,2,1,1,32,3072]{6,5,4,3,2,1,0:T(8,128)(2,1)S(1)}, bf16[1,1,2,1,1,32,3072]{6,5,4,3,2,1,0:T(8,128)(2,1)S(1)}, u32[]{:S(2)}, u32[]{:S(2)}) collective-permute-start(bf16[1,1,2,1,1,32,3072]{6,5,4,3,2,1,0:T(8,128)(2,1)S(1)} %pad_maximum_fusion.30), channel_id=1, source_target_pairs={{0,2},{1,3},{2,0},{3,1},{4,6},{5,7},{6,4},{7,5},{8,10},{9,11},{10,... | collective-permute-start | bytes 1179656 | tf_op jit(solution)/shard_map/ppermute | solution.py:244
  40.0 29.0 %collective-permute-start.25 = (bf16[1,1,1,2,1,128,1024]{6,5,4,3,2,1,0:T(8,128)(2,1)S(1)}, bf16[1,1,1,2,1,128,1024]{6,5,4,3,2,1,0:T(8,128)(2,1)S(1)}, u32[]{:S(2)}, u32[]{:S(2)}) collective-permute-start(bf16[1,1,1,2,1,128,1024]{6,5,4,3,2,1,0:T(8,128)(2,1)S(1)} %pad_maximum_fusion.27), channel_id=1, source_target_pairs={{0,16},{1,17},{2,18},{3,19},{4,20},{5,21},{6,22},{7,23},{8,24},{9,... | collective-permute-start | bytes 1572872 | tf_op jit(solution)/shard_map/ppermute | solution.py:244
  43.7 25.6 %collective-permute-start.19 = (bf16[2,1,1,1,1,32,4096]{6,5,4,3,2,1,0:T(8,128)(2,1)S(1)}, bf16[2,1,1,1,1,32,4096]{6,5,4,3,2,1,0:T(8,128)(2,1)S(1)}, u32[]{:S(2)}, u32[]{:S(2)}) collective-permute-start(bf16[2,1,1,1,1,32,4096]{6,5,4,3,2,1,0:T(8,128)(2,1)S(1)} %pad_maximum_fusion.26), channel_id=1, source_target_pairs={{0,8},{1,9},{2,10},{3,11},{4,12},{5,13},{6,14},{7,15},{8,0},{9,1},... | collective-permute-start | bytes 1572872 | tf_op jit(solution)/shard_map/ppermute | solution.py:244
  46.3 75.8 %collective-permute-start.16 = (bf16[2,2,2,1,1,32,1024]{6,5,4,3,2,1,0:T(8,128)(2,1)}, bf16[2,2,2,1,1,32,1024]{6,5,4,3,2,1,0:T(8,128)(2,1)}, u32[]{:S(2)}, u32[]{:S(2)}) collective-permute-start(bf16[2,2,2,1,1,32,1024]{6,5,4,3,2,1,0:T(8,128)(2,1)} %pad_maximum_fusion.25), channel_id=1, source_target_pairs={{0,1},{1,0},{2,3},{3,2},{4,5},{5,4},{6,7},{7,6},{8,9},{9,8},{10,11... | collective-permute-start | bytes 1572872 | tf_op jit(solution)/shard_map/ppermute | solution.py:244
  46.3 23.8 %collective-permute-start.15 = (bf16[2,2,2,1,1,32,1024]{6,5,4,3,2,1,0:T(8,128)(2,1)}, bf16[2,2,2,1,1,32,1024]{6,5,4,3,2,1,0:T(8,128)(2,1)}, u32[]{:S(2)}, u32[]{:S(2)}) collective-permute-start(bf16[2,2,2,1,1,32,1024]{6,5,4,3,2,1,0:T(8,128)(2,1)} %pad_maximum_fusion.25), channel_id=1, source_target_pairs={{0,2},{1,3},{2,0},{3,1},{4,6},{5,7},{6,4},{7,5},{8,10},{9,11},{10,... | collective-permute-start | bytes 1572872 | tf_op jit(solution)/shard_map/ppermute | solution.py:244
  48.9 50.9 %collective-permute-start.2 = (bf16[1,1,2,2,1,32,3072]{6,5,4,3,2,1,0:T(8,128)(2,1)S(1)}, bf16[1,1,2,2,1,32,3072]{6,5,4,3,2,1,0:T(8,128)(2,1)S(1)}, u32[]{:S(2)}, u32[]{:S(2)}) collective-permute-start(bf16[1,1,2,2,1,32,3072]{6,5,4,3,2,1,0:T(8,128)(2,1)S(1)} %pad_maximum_fusion.19), channel_id=1, source_target_pairs={{0,16},{1,17},{2,18},{3,19},{4,20},{5,21},{6,22},{7,23},{8,24},{9,... | collective-permute-start | bytes 2359304 | tf_op jit(solution)/shard_map/ppermute | solution.py:244
  69.2 40.9 %collective-permute-start.26 = (bf16[2,1,1,2,1,128,1024]{6,5,4,3,2,1,0:T(8,128)(2,1)S(1)}, bf16[2,1,1,2,1,128,1024]{6,5,4,3,2,1,0:T(8,128)(2,1)S(1)}, u32[]{:S(2)}, u32[]{:S(2)}) collective-permute-start(bf16[2,1,1,2,1,128,1024]{6,5,4,3,2,1,0:T(8,128)(2,1)S(1)} %pad_maximum_fusion.17), channel_id=1, source_target_pairs={{0,8},{1,9},{2,10},{3,11},{4,12},{5,13},{6,14},{7,15},{8,0},{9,1},... | collective-permute-start | bytes 3145736 | tf_op jit(solution)/shard_map/ppermute | solution.py:244
  69.5 43.3 %collective-permute-start.20 = (bf16[2,2,1,1,1,32,4096]{6,5,4,3,2,1,0:T(8,128)(2,1)S(1)}, bf16[2,2,1,1,1,32,4096]{6,5,4,3,2,1,0:T(8,128)(2,1)S(1)}, u32[]{:S(2)}, u32[]{:S(2)}) collective-permute-start(bf16[2,2,1,1,1,32,4096]{6,5,4,3,2,1,0:T(8,128)(2,1)S(1)} %pad_maximum_fusion.16), channel_id=1, source_target_pairs={{0,4},{1,5},{2,6},{3,7},{4,0},{5,1},{6,2},{7,3},{8,12},{9,13},{10,... | collective-permute-start | bytes 3145736 | tf_op jit(solution)/shard_map/ppermute | solution.py:244
  70.1 52.1 %collective-permute-start.17 = (bf16[2,2,2,1,1,32,1024]{6,5,4,3,2,1,0:T(8,128)(2,1)}, bf16[2,2,2,1,1,32,1024]{6,5,4,3,2,1,0:T(8,128)(2,1)}, u32[]{:S(2)}, u32[]{:S(2)}) collective-permute-start(bf16[2,2,2,1,1,32,1024]{6,5,4,3,2,1,0:T(8,128)(2,1)} %collective-permute-done.15), channel_id=1, source_target_pairs={{0,1},{1,0},{2,3},{3,2},{4,5},{5,4},{6,7},{7,6},{8,9},{9,8},{10,11... | collective-permute-start | bytes 1572872 | tf_op jit(solution)/shard_map/ppermute | solution.py:244
  101.4 39.0 %collective-permute-start.3 = (bf16[2,1,2,2,1,32,3072]{6,5,4,3,2,1,0:T(8,128)(2,1)}, bf16[2,1,2,2,1,32,3072]{6,5,4,3,2,1,0:T(8,128)(2,1)}, u32[]{:S(2)}, u32[]{:S(2)}) collective-permute-start(bf16[2,1,2,2,1,32,3072]{6,5,4,3,2,1,0:T(8,128)(2,1)} %pad_maximum_fusion.12), channel_id=1, source_target_pairs={{0,8},{1,9},{2,10},{3,11},{4,12},{5,13},{6,14},{7,15},{8,0},{9,1},... | collective-permute-start | bytes 4718600 | tf_op jit(solution)/shard_map/ppermute | solution.py:244
  112.1 40.6 %collective-permute-start.27 = (bf16[2,2,1,2,1,128,1024]{6,5,4,3,2,1,0:T(8,128)(2,1)}, bf16[2,2,1,2,1,128,1024]{6,5,4,3,2,1,0:T(8,128)(2,1)}, u32[]{:S(2)}, u32[]{:S(2)}) collective-permute-start(bf16[2,2,1,2,1,128,1024]{6,5,4,3,2,1,0:T(8,128)(2,1)} %pad_maximum_fusion.11), channel_id=1, source_target_pairs={{0,4},{1,5},{2,6},{3,7},{4,0},{5,1},{6,2},{7,3},{8,12},{9,13},{10,... | collective-permute-start | bytes 6291464 | tf_op jit(solution)/shard_map/ppermute | solution.py:244
  115.0 41.7 %collective-permute-start.21 = (bf16[2,2,2,1,1,32,4096]{6,5,4,3,2,1,0:T(8,128)(2,1)}, bf16[2,2,2,1,1,32,4096]{6,5,4,3,2,1,0:T(8,128)(2,1)}, u32[]{:S(2)}, u32[]{:S(2)}) collective-permute-start(bf16[2,2,2,1,1,32,4096]{6,5,4,3,2,1,0:T(8,128)(2,1)} %pad_maximum_fusion.10), channel_id=1, source_target_pairs={{0,2},{1,3},{2,0},{3,1},{4,6},{5,7},{6,4},{7,5},{8,10},{9,11},{10,... | collective-permute-start | bytes 6291464 | tf_op jit(solution)/shard_map/ppermute | solution.py:244
  122.1 156.3 %collective-permute-start.30 = (bf16[128,512]{0,1:T(8,128)(2,1)}, bf16[128,512]{0,1:T(8,128)(2,1)}, u32[]{:S(2)}, u32[]{:S(2)}) collective-permute-start(bf16[128,512]{0,1:T(8,128)(2,1)} %bitcast.24), channel_id=1, source_target_pairs={{0,1},{1,0},{2,3},{3,2},{4,5},{5,4},{6,7},{7,6},{8,9},{9,8},{10,11... | collective-permute-start | bytes 393224 | tf_op jit(solution)/shard_map/ppermute | solution.py:244
  122.2 39.1 %collective-permute-start.4 = (bf16[2,1,2,2,1,32,3072]{6,5,4,3,2,1,0:T(8,128)(2,1)}, bf16[2,1,2,2,1,32,3072]{6,5,4,3,2,1,0:T(8,128)(2,1)S(1)}, u32[]{:S(2)}, u32[]{:S(2)}) collective-permute-start(bf16[2,1,2,2,1,32,3072]{6,5,4,3,2,1,0:T(8,128)(2,1)} %pad_maximum_fusion.12), channel_id=1, source_target_pairs={{0,1},{1,0},{2,3},{3,2},{4,5},{5,4},{6,7},{7,6},{8,9},{9,8},{10,11... | collective-permute-start | bytes 4718600 | tf_op jit(solution)/shard_map/ppermute | solution.py:244
  140.4 20.9 %collective-permute-start.5 = (bf16[2,1,2,2,1,32,3072]{6,5,4,3,2,1,0:T(8,128)(2,1)}, bf16[2,1,2,2,1,32,3072]{6,5,4,3,2,1,0:T(8,128)(2,1)S(1)}, u32[]{:S(2)}, u32[]{:S(2)}) collective-permute-start(bf16[2,1,2,2,1,32,3072]{6,5,4,3,2,1,0:T(8,128)(2,1)} %collective-permute-done.3), channel_id=1, source_target_pairs={{0,1},{1,0},{2,3},{3,2},{4,5},{5,4},{6,7},{7,6},{8,9},{9,8},{10,11... | collective-permute-start | bytes 4718600 | tf_op jit(solution)/shard_map/ppermute | solution.py:244
  152.7 18.6 %collective-permute-start.28 = (bf16[2,2,1,2,1,128,1024]{6,5,4,3,2,1,0:T(8,128)(2,1)}, bf16[2,2,1,2,1,128,1024]{6,5,4,3,2,1,0:T(8,128)(2,1)}, u32[]{:S(2)}, u32[]{:S(2)}) collective-permute-start(bf16[2,2,1,2,1,128,1024]{6,5,4,3,2,1,0:T(8,128)(2,1)} %pad_maximum_fusion.11), channel_id=1, source_target_pairs={{0,1},{1,0},{2,3},{3,2},{4,5},{5,4},{6,7},{7,6},{8,9},{9,8},{10,11... | collective-permute-start | bytes 6291464 | tf_op jit(solution)/shard_map/ppermute | solution.py:244
  156.7 29.4 %collective-permute-start.22 = (bf16[2,2,2,1,1,32,4096]{6,5,4,3,2,1,0:T(8,128)(2,1)}, bf16[2,2,2,1,1,32,4096]{6,5,4,3,2,1,0:T(8,128)(2,1)}, u32[]{:S(2)}, u32[]{:S(2)}) collective-permute-start(bf16[2,2,2,1,1,32,4096]{6,5,4,3,2,1,0:T(8,128)(2,1)} %pad_maximum_fusion.10), channel_id=1, source_target_pairs={{0,1},{1,0},{2,3},{3,2},{4,5},{5,4},{6,7},{7,6},{8,9},{9,8},{10,11... | collective-permute-start | bytes 6291464 | tf_op jit(solution)/shard_map/ppermute | solution.py:244
  161.3 10.1 %collective-permute-start.29 = (bf16[2,2,1,2,1,128,1024]{6,5,4,3,2,1,0:T(8,128)(2,1)}, bf16[2,2,1,2,1,128,1024]{6,5,4,3,2,1,0:T(8,128)(2,1)}, u32[]{:S(2)}, u32[]{:S(2)}) collective-permute-start(bf16[2,2,1,2,1,128,1024]{6,5,4,3,2,1,0:T(8,128)(2,1)} %collective-permute-done.27), channel_id=1, source_target_pairs={{0,1},{1,0},{2,3},{3,2},{4,5},{5,4},{6,7},{7,6},{8,9},{9,8},{10,11... | collective-permute-start | bytes 6291464 | tf_op jit(solution)/shard_map/ppermute | solution.py:244
  161.3 24.8 %collective-permute-start.23 = (bf16[2,2,2,1,1,32,4096]{6,5,4,3,2,1,0:T(8,128)(2,1)}, bf16[2,2,2,1,1,32,4096]{6,5,4,3,2,1,0:T(8,128)(2,1)}, u32[]{:S(2)}, u32[]{:S(2)}) collective-permute-start(bf16[2,2,2,1,1,32,4096]{6,5,4,3,2,1,0:T(8,128)(2,1)} %collective-permute-done.21), channel_id=1, source_target_pairs={{0,1},{1,0},{2,3},{3,2},{4,5},{5,4},{6,7},{7,6},{8,9},{9,8},{10,11... | collective-permute-start | bytes 6291464 | tf_op jit(solution)/shard_map/ppermute | solution.py:244
  236.7 46.5 %collective-permute-start.55 = (bf16[128,512]{0,1:T(8,128)(2,1)}, bf16[128,512]{0,1:T(8,128)(2,1)}, u32[]{:S(2)}, u32[]{:S(2)}) collective-permute-start(bf16[128,512]{0,1:T(8,128)(2,1)} %bitcast.45), channel_id=1, source_target_pairs={{0,1},{1,0},{2,3},{3,2},{4,5},{5,4},{6,7},{7,6},{8,9},{9,8},{10,11... | collective-permute-start | bytes 393224 | tf_op jit(solution)/shard_map/ppermute | solution.py:244
  237.1 22.8 %collective-permute-start.49 = (bf16[128,512]{0,1:T(8,128)(2,1)}, bf16[128,512]{0,1:T(8,128)(2,1)}, u32[]{:S(2)}, u32[]{:S(2)}) collective-permute-start(bf16[128,512]{0,1:T(8,128)(2,1)} %bitcast.37), channel_id=1, source_target_pairs={{0,1},{1,0},{2,3},{3,2},{4,5},{5,4},{6,7},{7,6},{8,9},{9,8},{10,11... | collective-permute-start | bytes 393224 | tf_op jit(solution)/shard_map/ppermute | solution.py:244
  251.6 8.8 %collective-permute-start.50 = (bf16[128,1024]{1,0:T(8,128)(2,1)}, bf16[128,1024]{1,0:T(8,128)(2,1)}, u32[]{:S(2)}, u32[]{:S(2)}) collective-permute-start(bf16[128,1024]{1,0:T(8,128)(2,1)} %convert_element_type.463), channel_id=1, source_target_pairs={{0,1},{1,0},{2,3},{3,2},{4,5},{5,4},{6,7},{7,6},{8,9},{9,8},{10,11... | collective-permute-start | bytes 786440 | tf_op jit(solution)/shard_map/ppermute | solution.py:244
  262.2 22.7 %collective-permute-start.56 = (bf16[128,4096]{1,0:T(8,128)(2,1)S(1)}, bf16[128,4096]{1,0:T(8,128)(2,1)S(1)}, u32[]{:S(2)}, u32[]{:S(2)}) collective-permute-start(bf16[128,4096]{1,0:T(8,128)(2,1)S(1)} %copy-done.20), channel_id=1, source_target_pairs={{0,1},{1,0},{2,3},{3,2},{4,5},{5,4},{6,7},{7,6},{8,9},{9,8},{10,11... | collective-permute-start | bytes 3145736 | tf_op jit(solution)/shard_map/ppermute | solution.py:244
  262.7 13.9 %collective-permute-start.51 = (bf16[2,2,1,2,32,1024]{5,4,3,2,1,0:T(8,128)(2,1)S(1)}, bf16[2,2,1,2,32,1024]{5,4,3,2,1,0:T(8,128)(2,1)S(1)}, u32[]{:S(2)}, u32[]{:S(2)}) collective-permute-start(bf16[2,2,1,2,32,1024]{5,4,3,2,1,0:T(8,128)(2,1)S(1)} %constant_dynamic-slice_fusion.23), channel_id=1, source_target_pairs={{0,4},{1,5},{2,6},{3,7},{4,0},{5,1},{6,2},{7,3},{8,12},{9,13},{10,... | collective-permute-start | bytes 1572872 | tf_op jit(solution)/shard_map/ppermute | solution.py:244
  267.6 22.7 %collective-permute-start.71 = (bf16[2,1,2,2,128,256]{5,4,3,2,1,0:T(8,128)(2,1)S(1)}, bf16[2,1,2,2,128,256]{5,4,3,2,1,0:T(8,128)(2,1)S(1)}, u32[]{:S(2)}, u32[]{:S(2)}) collective-permute-start(bf16[2,1,2,2,128,256]{5,4,3,2,1,0:T(8,128)(2,1)S(1)} %constant_dynamic-slice_fusion.3), channel_id=1, source_target_pairs={{0,8},{1,9},{2,10},{3,11},{4,12},{5,13},{6,14},{7,15},{8,0},{9,1},... | collective-permute-start | bytes 1572872 | tf_op jit(solution)/shard_map/ppermute | solution.py:244
  276.6 111.2 %collective-permute-start.67 = (bf16[2,2,1,2,128,768]{5,4,3,2,1,0:T(8,128)(2,1)S(1)}, bf16[2,2,1,2,128,768]{5,4,3,2,1,0:T(8,128)(2,1)S(1)}, u32[]{:S(2)}, u32[]{:S(2)}) collective-permute-start(bf16[2,2,1,2,128,768]{5,4,3,2,1,0:T(8,128)(2,1)S(1)} %constant_dynamic-slice_fusion.7), channel_id=1, source_target_pairs={{0,4},{1,5},{2,6},{3,7},{4,0},{5,1},{6,2},{7,3},{8,12},{9,13},{10,... | collective-permute-start | bytes 4718600 | tf_op jit(solution)/shard_map/ppermute | solution.py:244
  278.4 10.5 %collective-permute-start.52 = (bf16[2,1,1,2,32,1024]{5,4,3,2,1,0:T(8,128)(2,1)S(1)}, bf16[2,1,1,2,32,1024]{5,4,3,2,1,0:T(8,128)(2,1)S(1)}, u32[]{:S(2)}, u32[]{:S(2)}) collective-permute-start(bf16[2,1,1,2,32,1024]{5,4,3,2,1,0:T(8,128)(2,1)S(1)} %constant_dynamic-slice_fusion.22), channel_id=1, source_target_pairs={{0,8},{1,9},{2,10},{3,11},{4,12},{5,13},{6,14},{7,15},{8,0},{9,1},... | collective-permute-start | bytes 786440 | tf_op jit(solution)/shard_map/ppermute | solution.py:244
  283.2 24.1 %collective-permute-start.40 = (bf16[2,1,2,2,32,1024]{5,4,3,2,1,0:T(8,128)(2,1)S(1)}, bf16[2,1,2,2,32,1024]{5,4,3,2,1,0:T(8,128)(2,1)S(1)}, u32[]{:S(2)}, u32[]{:S(2)}) collective-permute-start(bf16[2,1,2,2,32,1024]{5,4,3,2,1,0:T(8,128)(2,1)S(1)} %constant_dynamic-slice_fusion.38), channel_id=1, source_target_pairs={{0,8},{1,9},{2,10},{3,11},{4,12},{5,13},{6,14},{7,15},{8,0},{9,1},... | collective-permute-start | bytes 1572872 | tf_op jit(solution)/shard_map/ppermute | solution.py:244
  284.9 32.7 %collective-permute-start.32 = (bf16[2,2,2,1,32,1024]{5,4,3,2,1,0:T(8,128)(2,1)S(1)}, bf16[2,2,2,1,32,1024]{5,4,3,2,1,0:T(8,128)(2,1)S(1)}, u32[]{:S(2)}, u32[]{:S(2)}) collective-permute-start(bf16[2,2,2,1,32,1024]{5,4,3,2,1,0:T(8,128)(2,1)S(1)} %constant_dynamic-slice_fusion.46), channel_id=1, source_target_pairs={{0,2},{1,3},{2,0},{3,1},{4,6},{5,7},{6,4},{7,5},{8,10},{9,11},{10,... | collective-permute-start | bytes 1572872 | tf_op jit(solution)/shard_map/ppermute | solution.py:244
  288.9 34.5 %collective-permute-start.36 = (bf16[2,2,1,2,32,1024]{5,4,3,2,1,0:T(8,128)(2,1)S(1)}, bf16[2,2,1,2,32,1024]{5,4,3,2,1,0:T(8,128)(2,1)S(1)}, u32[]{:S(2)}, u32[]{:S(2)}) collective-permute-start(bf16[2,2,1,2,32,1024]{5,4,3,2,1,0:T(8,128)(2,1)S(1)} %constant_dynamic-slice_fusion.42), channel_id=1, source_target_pairs={{0,4},{1,5},{2,6},{3,7},{4,0},{5,1},{6,2},{7,3},{8,12},{9,13},{10,... | collective-permute-start | bytes 1572872 | tf_op jit(solution)/shard_map/ppermute | solution.py:244
  303.3 13.7 %collective-permute-start.72 = (bf16[1,1,2,2,128,256]{5,4,3,2,1,0:T(8,128)(2,1)S(1)}, bf16[1,1,2,2,128,256]{5,4,3,2,1,0:T(8,128)(2,1)S(1)}, u32[]{:S(2)}, u32[]{:S(2)}) collective-permute-start(bf16[1,1,2,2,128,256]{5,4,3,2,1,0:T(8,128)(2,1)S(1)} %constant_dynamic-slice_fusion.2), channel_id=1, source_target_pairs={{0,16},{1,17},{2,18},{3,19},{4,20},{5,21},{6,22},{7,23},{8,24},{9,... | collective-permute-start | bytes 786440 | tf_op jit(solution)/shard_map/ppermute | solution.py:244
  307.3 50.0 %collective-permute-start.61 = (bf16[2,1,2,2,32,1024]{5,4,3,2,1,0:T(8,128)(2,1)S(1)}, bf16[2,1,2,2,32,1024]{5,4,3,2,1,0:T(8,128)(2,1)S(1)}, u32[]{:S(2)}, u32[]{:S(2)}) collective-permute-start(bf16[2,1,2,2,32,1024]{5,4,3,2,1,0:T(8,128)(2,1)S(1)} %constant_dynamic-slice_fusion.13), channel_id=1, source_target_pairs={{0,8},{1,9},{2,10},{3,11},{4,12},{5,13},{6,14},{7,15},{8,0},{9,1},... | collective-permute-start | bytes 1572872 | tf_op jit(solution)/shard_map/ppermute | solution.py:244
  316.9 73.2 %collective-permute-start.57 = (bf16[2,2,2,1,32,3072]{5,4,3,2,1,0:T(8,128)(2,1)S(1)}, bf16[2,2,2,1,32,3072]{5,4,3,2,1,0:T(8,128)(2,1)S(1)}, u32[]{:S(2)}, u32[]{:S(2)}) collective-permute-start(bf16[2,2,2,1,32,3072]{5,4,3,2,1,0:T(8,128)(2,1)S(1)} %constant_dynamic-slice_fusion.17), channel_id=1, source_target_pairs={{0,2},{1,3},{2,0},{3,1},{4,6},{5,7},{6,4},{7,5},{8,10},{9,11},{10,... | collective-permute-start | bytes 4718600 | tf_op jit(solution)/shard_map/ppermute | solution.py:244
  317.6 34.4 %collective-permute-start.73 = (bf16[1,1,2,1,128,256]{5,4,3,2,1,0:T(8,128)(2,1)S(1)}, bf16[1,1,2,1,128,256]{5,4,3,2,1,0:T(8,128)(2,1)S(1)}, u32[]{:S(2)}, u32[]{:S(2)}) collective-permute-start(bf16[1,1,2,1,128,256]{5,4,3,2,1,0:T(8,128)(2,1)S(1)} %constant_dynamic-slice_fusion.1), channel_id=1, source_target_pairs={{0,2},{1,3},{2,0},{3,1},{4,6},{5,7},{6,4},{7,5},{8,10},{9,11},{10,... | collective-permute-start | bytes 393224 | tf_op jit(solution)/shard_map/ppermute | solution.py:244
  323.4 37.0 %collective-permute-start.41 = (bf16[1,1,2,2,32,1024]{5,4,3,2,1,0:T(8,128)(2,1)S(1)}, bf16[1,1,2,2,32,1024]{5,4,3,2,1,0:T(8,128)(2,1)S(1)}, u32[]{:S(2)}, u32[]{:S(2)}) collective-permute-start(bf16[1,1,2,2,32,1024]{5,4,3,2,1,0:T(8,128)(2,1)S(1)} %constant_dynamic-slice_fusion.37), channel_id=1, source_target_pairs={{0,16},{1,17},{2,18},{3,19},{4,20},{5,21},{6,22},{7,23},{8,24},{9,... | collective-permute-start | bytes 786440 | tf_op jit(solution)/shard_map/ppermute | solution.py:244
  357.3 13.8 %collective-permute-start.37 = (bf16[2,1,1,2,32,1024]{5,4,3,2,1,0:T(8,128)(2,1)S(1)}, bf16[2,1,1,2,32,1024]{5,4,3,2,1,0:T(8,128)(2,1)S(1)}, u32[]{:S(2)}, u32[]{:S(2)}) collective-permute-start(bf16[2,1,1,2,32,1024]{5,4,3,2,1,0:T(8,128)(2,1)S(1)} %constant_dynamic-slice_fusion.41), channel_id=1, source_target_pairs={{0,8},{1,9},{2,10},{3,11},{4,12},{5,13},{6,14},{7,15},{8,0},{9,1},... | collective-permute-start | bytes 786440 | tf_op jit(solution)/shard_map/ppermute | solution.py:244
  360.3 25.8 %collective-permute-start.62 = (bf16[1,1,2,2,32,1024]{5,4,3,2,1,0:T(8,128)(2,1)S(1)}, bf16[1,1,2,2,32,1024]{5,4,3,2,1,0:T(8,128)(2,1)S(1)}, u32[]{:S(2)}, u32[]{:S(2)}) collective-permute-start(bf16[1,1,2,2,32,1024]{5,4,3,2,1,0:T(8,128)(2,1)S(1)} %constant_dynamic-slice_fusion.12), channel_id=1, source_target_pairs={{0,16},{1,17},{2,18},{3,19},{4,20},{5,21},{6,22},{7,23},{8,24},{9,... | collective-permute-start | bytes 786440 | tf_op jit(solution)/shard_map/ppermute | solution.py:244
  371.2 9.7 %collective-permute-start.38 = (bf16[1,1,1,2,32,1024]{5,4,3,2,1,0:T(8,128)(2,1)S(1)}, bf16[1,1,1,2,32,1024]{5,4,3,2,1,0:T(8,128)(2,1)S(1)}, u32[]{:S(2)}, u32[]{:S(2)}) collective-permute-start(bf16[1,1,1,2,32,1024]{5,4,3,2,1,0:T(8,128)(2,1)S(1)} %constant_dynamic-slice_fusion.40), channel_id=1, source_target_pairs={{0,16},{1,17},{2,18},{3,19},{4,20},{5,21},{6,22},{7,23},{8,24},{9,... | collective-permute-start | bytes 393224 | tf_op jit(solution)/shard_map/ppermute | solution.py:244
  388.3 18.4 %collective-permute-start.68 = (bf16[2,1,1,2,128,768]{5,4,3,2,1,0:T(8,128)(2,1)S(1)}, bf16[2,1,1,2,128,768]{5,4,3,2,1,0:T(8,128)(2,1)S(1)}, u32[]{:S(2)}, u32[]{:S(2)}) collective-permute-start(bf16[2,1,1,2,128,768]{5,4,3,2,1,0:T(8,128)(2,1)S(1)} %constant_dynamic-slice_fusion.6), channel_id=1, source_target_pairs={{0,8},{1,9},{2,10},{3,11},{4,12},{5,13},{6,14},{7,15},{8,0},{9,1},... | collective-permute-start | bytes 2359304 | tf_op jit(solution)/shard_map/ppermute | solution.py:244
  390.9 19.1 %collective-permute-start.58 = (bf16[2,2,1,1,32,3072]{5,4,3,2,1,0:T(8,128)(2,1)S(1)}, bf16[2,2,1,1,32,3072]{5,4,3,2,1,0:T(8,128)(2,1)S(1)}, u32[]{:S(2)}, u32[]{:S(2)}) collective-permute-start(bf16[2,2,1,1,32,3072]{5,4,3,2,1,0:T(8,128)(2,1)S(1)} %constant_dynamic-slice_fusion.16), channel_id=1, source_target_pairs={{0,4},{1,5},{2,6},{3,7},{4,0},{5,1},{6,2},{7,3},{8,12},{9,13},{10,... | collective-permute-start | bytes 2359304 | tf_op jit(solution)/shard_map/ppermute | solution.py:244
  392.5 20.4 %collective-permute-start.64 = (bf16[1,1,1,1,32,1024]{5,4,3,2,1,0:T(8,128)(2,1)S(1)}, bf16[1,1,1,1,32,1024]{5,4,3,2,1,0:T(8,128)(2,1)S(1)}, u32[]{:S(2)}, u32[]{:S(2)}) collective-permute-start(bf16[1,1,1,1,32,1024]{5,4,3,2,1,0:T(8,128)(2,1)S(1)} %constant_dynamic-slice_fusion.10), channel_id=1, source_target_pairs={{0,4},{1,5},{2,6},{3,7},{4,0},{5,1},{6,2},{7,3},{8,12},{9,13},{10,... | collective-permute-start | bytes 196616 | tf_op jit(solution)/shard_map/ppermute | solution.py:244
  407.0 17.2 %collective-permute-start.69 = (bf16[1,1,1,2,128,768]{5,4,3,2,1,0:T(8,128)(2,1)S(1)}, bf16[1,1,1,2,128,768]{5,4,3,2,1,0:T(8,128)(2,1)S(1)}, u32[]{:S(2)}, u32[]{:S(2)}) collective-permute-start(bf16[1,1,1,2,128,768]{5,4,3,2,1,0:T(8,128)(2,1)S(1)} %constant_dynamic-slice_fusion.5), channel_id=1, source_target_pairs={{0,16},{1,17},{2,18},{3,19},{4,20},{5,21},{6,22},{7,23},{8,24},{9,... | collective-permute-start | bytes 1179656 | tf_op jit(solution)/shard_map/ppermute | solution.py:244
  410.2 14.6 %collective-permute-start.59 = (bf16[2,1,1,1,32,3072]{5,4,3,2,1,0:T(8,128)(2,1)S(1)}, bf16[2,1,1,1,32,3072]{5,4,3,2,1,0:T(8,128)(2,1)S(1)}, u32[]{:S(2)}, u32[]{:S(2)}) collective-permute-start(bf16[2,1,1,1,32,3072]{5,4,3,2,1,0:T(8,128)(2,1)S(1)} %constant_dynamic-slice_fusion.15), channel_id=1, source_target_pairs={{0,8},{1,9},{2,10},{3,11},{4,12},{5,13},{6,14},{7,15},{8,0},{9,1},... | collective-permute-start | bytes 1179656 | tf_op jit(solution)/shard_map/ppermute | solution.py:244
  424.9 8.7 %collective-permute-start.60 = (bf16[1,1,1,1,32,3072]{5,4,3,2,1,0:T(8,128)(2,1)S(1)}, bf16[1,1,1,1,32,3072]{5,4,3,2,1,0:T(8,128)(2,1)S(1)}, u32[]{:S(2)}, u32[]{:S(2)}) collective-permute-start(bf16[1,1,1,1,32,3072]{5,4,3,2,1,0:T(8,128)(2,1)S(1)} %constant_dynamic-slice_fusion.14), channel_id=1, source_target_pairs={{0,16},{1,17},{2,18},{3,19},{4,20},{5,21},{6,22},{7,23},{8,24},{9,... | collective-permute-start | bytes 589832 | tf_op jit(solution)/shard_map/ppermute | solution.py:244
  (97 other events, 544.9 us)
